TPU v7x, 32 devices: a whole 2x2x4 slice. The times are simulated.
32 devices in a mesh: rows: 8 (over z, x), rep: 4 (over y, core).
Axes of the slice: x: 2, y: 2, z: 4, core: 2. Of those that a mesh axis runs over, the one named last changes fastest.
Arguments:
- right_side: float32 [32768, 1024], P(('rep', 'rows')), parts along dimension 0, may hold values from -6 to 6
- leaf_inverse: float32 [32768, 256], P(('rep', 'rows')), parts along dimension 0, may hold values from -0.375 to 0.375
- left_factors: float32 [5, 32768, 64], P(None, ('rep', 'rows')), parts along dimension 1, may hold values from -0.75 to 0.75
- right_factors: float32 [5, 32768, 64], P(None, ('rep', 'rows')), parts along dimension 1, may hold values from -0.4375 to 0.4375, as said below
- cores: float32 [124, 128, 128], P('rep'), parts along dimension 0, may hold values from -0.5 to 0.5
Outputs:
- solution: float32 [32768, 1024], P(('rep', 'rows')), parts along dimension 0
There are 4 independent parts, one for each index of `rep`. A program takes and returns all parts, laid end to end along the dimension named above; each array names one. Nothing has to cross between parts.
Inputs may be any that keep to these rules, and one draw needn't show every extreme that they name: `right_factors`: level j's entries are of order (8192 / 2^(j+1))^(-1/2).
All inputs are finite; a program needn't handle non-finite values.
Results may differ from a plain program's by a relative error of at most 0.00016.
Values sent between devices are 32-bit elements; how exact they have to be, the bound alone decides.
A program may use at most 128 MiB of HBM per device.

v0:
```python
import functools

import jax
import jax.numpy as jnp
from jax import lax
from jax.experimental import pallas as pl
from jax.experimental.pallas import tpu as pltpu
from jax.sharding import PartitionSpec as P

LANES = 128
CHUNK = 2 * LANES
F32 = jnp.float32
TREE_VMEM = 24 << 20
APPLY_VMEM = 12 << 20


def split(x):
    high = x.astype(jnp.bfloat16)
    return high, (x - high.astype(F32)).astype(jnp.bfloat16)


def level_order(bits, levels):
    return [bits - 1 - s for s in range(bits)] + list(range(bits, levels))


def local_offset(level, bits, rank):
    return rank * (2 ** (level - bits + 1) - 2)


def dot3(a, b, nt=False):
    dims = (((1,), (1 if nt else 0,)), ((), ()))

    def one(x, y):
        return lax.dot_general(x, y, dims, preferred_element_type=F32)

    return one(a[0], b[0]) + one(a[0], b[1]) + one(a[1], b[0])


def dot(a, b):
    return dot3(split(a), split(b))


def tree_kernel(bits, levels, blocks, right_hbm, leaf_hbm, vt_hbm, ut_hbm, cores_hbm, *refs):
    x_hbm, qg_hbm, uh_hbm, ul_hbm = refs[:4]
    rbuf, leaf, vt_ref, ut_ref, core_g, sem_in, sem_out = refs[4:11]
    r_high, r_low, a_high, a_low, m_high, m_low, u_high, u_low, ql_ref, q_first = refs[11:21]
    gram_out, gram_in, first_out, first_in, later_out, later_in, q_out = refs[21:28]
    gram_sem, first_sem, later_sem, q_sem = refs[28:32]
    last_in, last_q, last_sem = refs[32:35]
    local_levels = list(range(bits, levels))
    core_l = refs[35 : 35 + len(local_levels)]
    ch_refs = refs[35 + len(local_levels) :]
    ch_refs = list(zip(ch_refs[::2], ch_refs[1::2]))

    me = lax.axis_index("rows")
    rank, rows_dev = vt_ref.shape[1:]
    chunks = rbuf.shape[0]
    lf = rows_dev // blocks
    half_id = lax.rem(me, 2)
    upper = half_id == 1
    order = level_order(bits, levels)

    def child(s):
        return lax.rem(me // 2**s, 2)

    def partner(s):
        return me + (1 - 2 * child(s)) * 2**s

    cross = partner(bits - 1) + (1 - 2 * child(0))
    barrier = pltpu.get_barrier_semaphore()
    for target in [partner(s) for s in range(bits)] + [cross]:
        pl.semaphore_signal(
            barrier, inc=1, device_id={"rows": target}, device_id_type=pl.DeviceIdType.MESH
        )

    slots = {"in": 0, "out": 0}

    def move(src, dst, sems, kind):
        copy = pltpu.make_async_copy(src, dst, sems.at[slots[kind]])
        slots[kind] += 1
        copy.start()
        return copy

    factor_loads = [move(vt_hbm, vt_ref, sem_in, "in"), move(ut_hbm, ut_ref, sem_in, "in")]
    leaf_load = move(leaf_hbm, leaf, sem_in, "in")
    core_loads = []
    for n, level in enumerate(local_levels):
        count = 2 ** (level - bits)
        src = cores_hbm.at[pl.ds(2**level - 1 + me * count, count)]
        core_loads.append(move(src, core_l[n], sem_in, "in"))
    right_loads = [
        move(right_hbm.at[:, pl.ds(c * CHUNK, CHUNK)], rbuf.at[c], sem_in, "in")
        for c in range(chunks)
    ]
    core_g_loads = []
    for s in range(bits):
        src = cores_hbm.at[2 ** (bits - 1 - s) - 1 + me // 2 ** (s + 1)]
        core_g_loads.append(move(src, core_g.at[s], sem_in, "in"))

    sent, written = [], []

    def send(src, dst, sems, s, target=None):
        copy = pltpu.make_async_remote_copy(
            src_ref=src,
            dst_ref=dst,
            send_sem=sems.at[0],
            recv_sem=sems.at[1],
            device_id={"rows": partner(s) if target is None else target},
            device_id_type=pl.DeviceIdType.MESH,
        )
        copy.start()
        sent.append(copy)
        return copy

    for copy in factor_loads:
        copy.wait()
    gram_cols = gram_out.shape[2]
    vt = split(jnp.concatenate([vt_ref[level] for level in order], 0))
    ut = split(jnp.concatenate([ut_ref[level] for level in order], 0))
    v_rows = [v[rank : rank * bits] for v in vt]
    u_rows = [u[:gram_cols] for u in ut]
    gram_out[0] = dot3(v_rows, u_rows, nt=True)
    pl.semaphore_wait(barrier, bits + 1)
    gram_copy = {0: send(gram_out.at[0], gram_in.at[0], gram_sem.at[0], 0)}

    for copy in core_loads:
        copy.wait()
    for n, level in enumerate(local_levels):
        count = 2 ** (level - bits)
        node = rows_dev // count
        half = node // 2
        zero = jnp.zeros((rank, half), jnp.bfloat16)
        own = slice(rank * level, rank * (level + 1))
        for k in range(count):
            base = k * node
            diag = [
                jnp.concatenate(
                    [
                        jnp.concatenate([u[own, base : base + half], zero], 1),
                        jnp.concatenate([zero, u[own, base + half : base + node]], 1),
                    ],
                    0,
                )
                for u in ut
            ]
            gram = dot3([v[: rank * level, base : base + node] for v in vt], diag, nt=True)
            core = core_l[n][k]
            for ref, top, rest in zip(ch_refs[n], split(core), split(dot(gram, core))):
                ref[k, : 2 * rank] = top
                ref[k, 2 * rank :] = rest
    leaf_load.wait()
    high, low = split(leaf[...])
    a_high[:, :lf] = high
    a_low[:, :lf] = low
    for i in range(blocks):
        rows = slice(i * lf, (i + 1) * lf)
        high, low = split(
            dot3([v[:, rows] for v in vt], (a_high[rows, :lf], a_low[rows, :lf]))
        )
        m_high[i] = high
        m_low[i] = low

    first_copy, later_copy, q_copy, last_copy = {}, {}, {}, {}

    def forward(c):
        right_loads[c].wait()
        high, low = split(rbuf[c])
        r_high[c] = high
        r_low[c] = low
        parts, later = [], []
        for i in range(blocks):
            rows = slice(i * lf, (i + 1) * lf)
            parts.append(dot3((m_high[i], m_low[i]), (r_high[c, rows, :], r_low[c, rows, :])))
        for n in reversed(range(len(local_levels))):
            level = local_levels[n]
            top = rank * level
            merged = []
            for k in range(len(parts) // 2):
                a, b = parts[2 * k], parts[2 * k + 1]
                both = split(jnp.concatenate([b[top:], a[top:]], 0))
                change = dot3([ref[k, 2 * rank :] for ref in ch_refs[n]], both)
                start = local_offset(level, bits, rank) + 2 * rank * k
                later.append((start, n, k, both))
                merged.append(a[:top] + b[:top] - change)
            parts = merged
        p = parts[0]
        low, high = p[:, :LANES], p[:, LANES:]
        first_out[c, :rank] = low[:rank]
        first_out[c, rank : 2 * rank] = high[:rank]
        first_out[c, 2 * rank :] = jnp.where(upper, low[rank:], high[rank:])
        first_copy[c] = send(first_out.at[c], first_in.at[c], first_sem.at[c], 0)
        later_out[0, c] = jnp.where(upper, high[rank:], low[rank:])
        for start, n, k, both in later:
            ql_ref[c, start : start + 2 * rank] = dot3(
                [ref[k, : 2 * rank] for ref in ch_refs[n]], both
            )

    def bases():
        if local_levels:
            rows = [ut_ref[level] for level in local_levels]
            extra = a_high.shape[1] - lf - rank * len(rows)
            if extra:
                rows.append(jnp.zeros((extra, rows_dev), F32))
            high, low = split(-jnp.concatenate(rows, 0).T)
            a_high[:, lf:] = high
            a_low[:, lf:] = low
        rows = [ut_ref[bits - 1 - s] for s in range(bits)]
        extra = u_high.shape[1] - rank * bits
        if extra:
            rows.append(jnp.zeros((extra, rows_dev), F32))
        high, low = split(-jnp.concatenate(rows, 0).T)
        u_high[...] = high
        u_low[...] = low
        written.append(move(u_high, uh_hbm, sem_out, "out"))
        written.append(move(u_low, ul_hbm, sem_out, "out"))

    def leaves(c):
        for i in range(blocks):
            rows = slice(i * lf, (i + 1) * lf)
            highs, lows = [r_high[c, rows, :]], [r_low[c, rows, :]]
            width = lf
            for level in local_levels:
                place = rank * (i * 2 ** (level - bits + 1) // blocks)
                start = local_offset(level, bits, rank) + place
                high, low = split(ql_ref[c, start : start + rank])
                highs.append(high)
                lows.append(low)
                width += rank
            if a_high.shape[1] > width:
                zero = jnp.zeros((a_high.shape[1] - width, CHUNK), jnp.bfloat16)
                highs.append(zero)
                lows.append(zero)
            rbuf[c, rows, :] = dot3(
                (a_high[rows, :], a_low[rows, :]),
                (jnp.concatenate(highs, 0), jnp.concatenate(lows, 0)),
            )
        written.append(move(rbuf.at[c], x_hbm.at[:, pl.ds(c * CHUNK, CHUNK)], sem_out, "out"))

    def stack(mine, theirs, s):
        first = child(s) == 0
        return jnp.concatenate([jnp.where(first, theirs, mine), jnp.where(first, mine, theirs)], 0)

    def pick(image, s):
        first = child(s) == 0
        return (
            jnp.where(first, image[:rank], image[rank:]),
            jnp.where(first, image[rank:], image[:rank]),
        )

    def correction(s, own, sib):
        zeros = [jnp.zeros((rank, LANES), F32)]
        before, after = s, gram_cols // rank - 1 - s
        rows = slice(rank * s, None)
        q_own = jnp.concatenate(zeros * before + [own] + zeros * after, 0)
        q_sib = jnp.concatenate(zeros * before + [sib] + zeros * after, 0)
        return dot(gram_out[s, rows, :], q_own) + dot(gram_in[s, rows, :], q_sib)

    def grams(s):
        gram_copy[s].wait_recv()
        if s + 1 < bits - 1:
            gram_out[s + 1] = gram_out[s] + gram_in[s]
            gram_copy[s + 1] = send(
                gram_out.at[s + 1], gram_in.at[s + 1], gram_sem.at[s + 1], s + 1
            )

    def last_step(s, c):
        later_copy[s, c].wait_recv()
        last_copy[0].wait_recv()
        last_copy[1].wait_recv()
        live = slice(rank * (s - 1), rank * s)

        def join(here, there):
            return jnp.concatenate(
                [jnp.where(upper, there, here), jnp.where(upper, here, there)], 1
            )

        mine = join(later_out[s, c, live], last_in[0])
        theirs = join(later_in[s, c, live], last_in[1])
        last_q[...] = pick(dot(core_g[s], stack(mine, theirs, s)), s)[0]
        target = qg_hbm.at[pl.ds(s * rank, rank), pl.ds(c * CHUNK, CHUNK)]
        written.append(move(last_q, target, sem_out, "out"))

    def step(s, c):
        if c == 0:
            core_g_loads[s].wait()
        if s == bits - 1 and c == chunks - 1:
            last_step(s, c)
            return
        if s == 0:
            first_copy[c].wait_recv()
            mine = jnp.concatenate([first_out[c, :rank], first_out[c, rank : 2 * rank]], 1)
            theirs = jnp.concatenate([first_in[c, :rank], first_in[c, rank : 2 * rank]], 1)
            image = dot(core_g[0], stack(mine, theirs, 0))
            own, sib = pick(image, 0)
            q_first[c] = own
            own = jnp.where(upper, own[:, LANES:], own[:, :LANES])
            sib = jnp.where(upper, sib[:, LANES:], sib[:, :LANES])
            rest = later_out[0, c] + first_in[c, 2 * rank :]
        else:
            later_copy[s, c].wait_recv()
            live = slice(rank * (s - 1), rank * s)
            image = dot(core_g[s], stack(later_out[s, c, live], later_in[s, c, live], s))
            own, sib = pick(image, s)
            q_out[s - 1, c] = own
            start = pl.multiple_of(c * CHUNK + half_id * LANES, LANES)
            target = qg_hbm.at[pl.ds(s * rank, rank), pl.ds(start, LANES)]
            q_copy[s, c] = send(q_out.at[s - 1, c], target, q_sem.at[s - 1, c], 0)
            if s < bits - 1:
                rest = later_out[s, c, rank * s :] + later_in[s, c, rank * s :]
        if s < bits - 1:
            later_out[s + 1, c, rank * s :] = rest - correction(s, own, sib)
            if s == bits - 2 and c == chunks - 1:
                root = later_out.at[s + 1, c, pl.ds(rank * s, rank)]
                last_copy[1] = send(root, last_in.at[1], last_sem.at[1], None, cross)
                last_copy[0] = send(root, last_in.at[0], last_sem.at[0], 0)
            later_copy[s + 1, c] = send(
                later_out.at[s + 1, c, pl.ds(rank * s, rank * (bits - 1 - s))],
                later_in.at[s + 1, c, pl.ds(rank * s, rank * (bits - 1 - s))],
                later_sem.at[s, c],
                s + 1,
            )
        if s == 0:
            target = qg_hbm.at[pl.ds(0, rank), pl.ds(c * CHUNK, CHUNK)]
            written.append(move(q_first.at[c], target, sem_out, "out"))
        else:
            written.append(move(q_out.at[s - 1, c], target, sem_out, "out"))

    for c in range(chunks):
        forward(c)
        if c == 0:
            grams(0)
    for s in range(1, bits - 1):
        grams(s)
    bases()
    for t in range(chunks + bits - 1):
        for s in range(bits):
            c = t - s
            if 0 <= c < chunks:
                step(s, c)
        if t < chunks:
            leaves(t)
    for copy in q_copy.values():
        copy.wait_recv()
    for copy in written:
        copy.wait()
    for copy in sent:
        copy.wait_send()


def tree(bits, right_side, leaf_inverse, vt, ut, cores):
    rows_dev, cols = right_side.shape
    lf = leaf_inverse.shape[1]
    levels, rank = vt.shape[:2]
    blocks = rows_dev // lf
    chunks = cols // CHUNK
    local_levels = list(range(bits, levels))
    assert blocks == 2 ** len(local_levels) and bits >= 2
    gram_cols = pl.cdiv(rank * (bits - 1), LANES) * LANES
    depth = lf + pl.cdiv(rank * len(local_levels), LANES) * LANES
    wide = pl.cdiv(rank * bits, LANES) * LANES
    out_shape = [
        jax.ShapeDtypeStruct((rows_dev, cols), F32),
        jax.ShapeDtypeStruct((rank * bits, cols), F32),
        jax.ShapeDtypeStruct((rows_dev, wide), jnp.bfloat16),
        jax.ShapeDtypeStruct((rows_dev, wide), jnp.bfloat16),
    ]
    hbm = pl.BlockSpec(memory_space=pltpu.HBM)
    free = pl.BlockSpec(memory_space=pl.ANY)
    counts = [2 ** (level - bits) for level in local_levels]
    rest = rank * (bits - 1)
    half = jnp.bfloat16
    scratch = [
        pltpu.VMEM((chunks, rows_dev, CHUNK), F32),
        pltpu.VMEM((rows_dev, lf), F32),
        pltpu.VMEM((levels, rank, rows_dev), F32),
        pltpu.VMEM((levels, rank, rows_dev), F32),
        pltpu.VMEM((bits, 2 * rank, 2 * rank), F32),
        pltpu.SemaphoreType.DMA((3 + levels + chunks,)),
        pltpu.SemaphoreType.DMA((2 + chunks * (bits + 1),)),
        pltpu.VMEM((chunks, rows_dev, CHUNK), half),
        pltpu.VMEM((chunks, rows_dev, CHUNK), half),
        pltpu.VMEM((rows_dev, depth), half),
        pltpu.VMEM((rows_dev, depth), half),
        pltpu.VMEM((blocks, levels * rank, lf), half),
        pltpu.VMEM((blocks, levels * rank, lf), half),
        pltpu.VMEM((rows_dev, wide), half),
        pltpu.VMEM((rows_dev, wide), half),
        pltpu.VMEM((chunks, max(rank * (2 * blocks - 2), rank), CHUNK), F32),
        pltpu.VMEM((chunks, rank, CHUNK), F32),
        pltpu.VMEM((bits - 1, rest, gram_cols), F32),
        pltpu.VMEM((bits - 1, rest, gram_cols), F32),
        pltpu.VMEM((chunks, 2 * rank + rest, LANES), F32),
        pltpu.VMEM((chunks, 2 * rank + rest, LANES), F32),
        pltpu.VMEM((bits, chunks, rest, LANES), F32),
        pltpu.VMEM((bits, chunks, rest, LANES), F32),
        pltpu.VMEM((bits - 1, chunks, rank, LANES), F32),
        pltpu.SemaphoreType.DMA((bits - 1, 2)),
        pltpu.SemaphoreType.DMA((chunks, 2)),
        pltpu.SemaphoreType.DMA((bits - 1, chunks, 2)),
        pltpu.SemaphoreType.DMA((bits - 1, chunks, 2)),
        pltpu.VMEM((2, rank, LANES), F32),
        pltpu.VMEM((rank, CHUNK), F32),
        pltpu.SemaphoreType.DMA((2, 2)),
    ]
    scratch += [pltpu.VMEM((count, 2 * rank, 2 * rank), F32) for count in counts]
    scratch += [
        pltpu.VMEM((count, rank * (level + 2), 2 * rank), half)
        for count, level in zip(counts, local_levels)
        for _ in range(2)
    ]
    return pl.pallas_call(
        functools.partial(tree_kernel, bits, levels, blocks),
        out_shape=out_shape,
        in_specs=[hbm] * 5,
        out_specs=[free] * 4,
        scratch_shapes=scratch,
        compiler_params=pltpu.CompilerParams(
            collective_id=0, has_side_effects=True, vmem_limit_bytes=TREE_VMEM + 32 * rows_dev * lf
        ),
        name="tree",
    )(right_side, leaf_inverse, vt, ut, cores)


def apply_kernel(x_ref, uh_ref, ul_ref, q_ref, out_ref):
    pad = uh_ref.shape[1] - q_ref.shape[0]
    q = q_ref[...]
    if pad:
        q = jnp.concatenate([q, jnp.zeros((pad, q.shape[1]), F32)], 0)
    high, low = split(q)
    out_ref[...] = x_ref[...] + dot3((uh_ref[...], ul_ref[...]), (high, low))


def apply(x, q, u_high, u_low):
    rows_dev, cols = x.shape
    width = CHUNK

    def column(rows):
        return pl.BlockSpec((rows, width), lambda c: (0, c))

    whole = pl.BlockSpec(u_high.shape, lambda c: (0, 0))
    return pl.pallas_call(
        apply_kernel,
        grid=(cols // width,),
        out_shape=jax.ShapeDtypeStruct((rows_dev, cols), F32),
        in_specs=[column(rows_dev), whole, whole, column(q.shape[0])],
        out_specs=column(rows_dev),
        compiler_params=pltpu.CompilerParams(vmem_limit_bytes=APPLY_VMEM),
        name="apply",
    )(x, u_high, u_low, q)


def local(bits, right_side, leaf_inverse, left_factors, right_factors, cores):
    ut = jnp.swapaxes(left_factors, 1, 2)
    vt = jnp.swapaxes(right_factors, 1, 2)
    right_side, leaf_inverse, vt, ut, cores = (
        pltpu.with_memory_space_constraint(a, pltpu.HBM)
        for a in (right_side, leaf_inverse, vt, ut, cores)
    )
    x, q, u_high, u_low = tree(bits, right_side, leaf_inverse, vt, ut, cores)
    return apply(x, q, u_high, u_low)


def solution(mesh):
    bits = mesh.shape["rows"].bit_length() - 1
    in_specs = (
        P(("rep", "rows"), None),
        P(("rep", "rows"), None),
        P(None, ("rep", "rows"), None),
        P(None, ("rep", "rows"), None),
        P("rep", None, None),
    )
    out_specs = P(("rep", "rows"), None)
    return jax.shard_map(
        functools.partial(local, bits),
        mesh=mesh,
        in_specs=in_specs,
        out_specs=out_specs,
        check_vma=False,
    )
```

profile of v0, /device:TPU:0, one launch (start us, length us, event | category | flops | bytes accessed | tf_op | source)
XLA Modules:
  0.0 37.5 jit_solution(11620274225088377839)
XLA Ops:
  0.0 33.5 %tree.1 = (f32[1024,1024]{1,0:T(8,128)S(1)}, f32[192,1024]{1,0:T(8,128)S(1)}, bf16[1024,256]{1,0:T(8,128)(2,1)S(1)}, bf16[1024,256]{1,0:T(8,128)(2,1)S(1)}) custom-call(f32[1024,1024]{1,0:T(8,128)} %right_hbm.1, f32[1024,256]{1,0:T(8,128)} %leaf_hbm.1, f32[5,64,1024]{2,1,0:T(8,128)} %bitcast.2, f32[5,64,1024]{2,1,0:T(8,128)} %bitcast.3, ...), custom_call_target="tpu_custom_call" | custom-call | tf_op jit(solution)/shard_map/tree/pallas_call | solution.py:411
  33.5 4.0 %apply.1 = f32[1024,1024]{1,0:T(8,128)} custom-call(f32[1024,1024]{1,0:T(8,128)S(1)} %get-tuple-element.9.x_ref, bf16[1024,256]{1,0:T(8,128)(2,1)S(1)} %get-tuple-element.10.uh_ref, bf16[1024,256]{1,0:T(8,128)(2,1)S(1)} %get-tuple-element.11.ul_ref, f32[192,1024]{1,0:T(8,128)S(1)} %get-tuple-element.12.q_ref), custom_call_target="tpu_custom_call" | custom-call | tf_op jit(solution)/shard_map/apply/pallas_call | solution.py:441
where the time goes:
time: 37.6 us; the launch traced here: 37.5 us
  Pallas kernels  37.5 us (100%)
    pallas_call x1, Pallas kernels, tree(): pl.pallas_call(functools.partial(tree_kernel, bits, levels, blocks), out_...  33.5 us
    pallas_call x1, Pallas kernels, apply(): pl.pallas_call(apply_kernel, grid=(cols // width,), out_shape=jax.ShapeDt...  3.99 us

commit v1 on v0

v1 whole, which is shorter than its diff:
```python
import contextlib
import functools

import jax
import jax.numpy as jnp
from jax import lax
from jax.experimental import pallas as pl
from jax.experimental.pallas import tpu as pltpu
from jax.sharding import PartitionSpec as P

LANES = 128
CHUNK = 2 * LANES
F32 = jnp.float32
BF16 = jnp.bfloat16
TREE_VMEM = 24 << 20
FINISH_VMEM = 12 << 20
MESH = pl.DeviceIdType.MESH
TRACE = False


def region(name):
    return jax.named_scope(name) if TRACE else contextlib.nullcontext()


def split(x):
    high = x.astype(BF16)
    return high, (x - high.astype(F32)).astype(BF16)


def level_order(bits, levels):
    return [bits - 1 - s for s in range(bits)] + list(range(bits, levels))


def local_offset(level, bits, rank):
    return rank * (2 ** (level - bits + 1) - 2)


def one(x, y, nt=False):
    dims = (((1,), (1 if nt else 0,)), ((), ()))
    return lax.dot_general(x, y, dims, preferred_element_type=F32)


def dot3(a, b, nt=False):
    return one(a[0], b[0], nt) + one(a[0], b[1], nt) + one(a[1], b[0], nt)


def dotk(a, b):
    return one(
        jnp.concatenate([a[0], a[0], a[1]], 1), jnp.concatenate([b[0], b[1], b[0]], 0)
    )


def dot(a, b):
    return dotk(split(a), split(b))


def swap_lanes(x):
    half = x.shape[1] // 2
    return jnp.concatenate([x[:, half:], x[:, :half]], 1)


def schedule(bits, chunks):
    if bits == 3 and chunks == 4:
        return [
            ("step", 0, 0), ("leaves", 0), ("step", 0, 1), ("leaves", 1),
            ("step", 1, 0), ("step", 0, 2), ("leaves", 2), ("step", 1, 1),
            ("step", 0, 3), ("step", 2, 0), ("step", 1, 2), ("leaves", 3),
            ("step", 2, 1), ("step", 1, 3), ("apply", 0), ("step", 2, 2),
            ("apply", 1), ("step", 2, 3), ("apply", 2),
        ]
    order = []
    for t in range(chunks + bits - 1):
        for s in range(bits):
            if 0 <= t - s < chunks:
                order.append(("step", s, t - s))
        if t < chunks:
            order.append(("leaves", t))
    return order + [("apply", c) for c in range(chunks - 1)]


def tree_kernel(bits, levels, blocks, right_hbm, leaf_hbm, vt_hbm, ut_hbm, cores_hbm, *refs):
    x_ref, q_last, u_high, u_low = refs[:4]
    rbuf, leaf, vt_ref, ut_ref, core_g, sem_in = refs[4:10]
    r_high, r_low, a_high, a_low, m_high, m_low, ql_ref = refs[10:17]
    op_high, op_low, gram_out, gram_in, keep, first_out, first_in = refs[17:24]
    later_out, later_in, q_out, q_all = refs[24:28]
    gram_sem, first_sem, later_sem, q_sem = refs[28:32]
    local_levels = list(range(bits, levels))
    core_l = refs[32 : 32 + len(local_levels)]
    ch_refs = refs[32 + len(local_levels) :]
    ch_refs = list(zip(ch_refs[::2], ch_refs[1::2]))

    me = lax.axis_index("rows")
    rank, rows_dev = vt_ref.shape[1:]
    chunks = rbuf.shape[0]
    lf = rows_dev // blocks
    half_id = lax.rem(me, 2)
    upper = half_id == 1
    order = level_order(bits, levels)
    gram_cols = gram_out.shape[2]

    def child(s):
        return lax.rem(me // 2**s, 2)

    def partner(s):
        return me + (1 - 2 * child(s)) * 2**s

    barrier = pltpu.get_barrier_semaphore()
    for s in range(bits):
        pl.semaphore_signal(
            barrier, inc=1, device_id={"rows": partner(s)}, device_id_type=MESH
        )

    slots = [0]

    def load(src, dst):
        copy = pltpu.make_async_copy(src, dst, sem_in.at[slots[0]])
        slots[0] += 1
        copy.start()
        return copy

    v_load = load(vt_hbm, vt_ref)
    leaf_load = load(leaf_hbm, leaf)
    u_load = load(ut_hbm, ut_ref)
    core_loads = []
    for n, level in enumerate(local_levels):
        count = 2 ** (level - bits)
        src = cores_hbm.at[pl.ds(2**level - 1 + me * count, count)]
        core_loads.append(load(src, core_l[n]))
    right_loads = [
        load(right_hbm.at[:, pl.ds(c * CHUNK, CHUNK)], rbuf.at[c]) for c in range(chunks)
    ]
    core_g_loads = []
    for s in range(bits):
        src = cores_hbm.at[2 ** (bits - 1 - s) - 1 + me // 2 ** (s + 1)]
        core_g_loads.append(load(src, core_g.at[s]))

    sent = []

    def send(src, dst, sems, s):
        copy = pltpu.make_async_remote_copy(
            src_ref=src,
            dst_ref=dst,
            send_sem=sems.at[0],
            recv_sem=sems.at[1],
            device_id={"rows": partner(s)},
            device_id_type=MESH,
        )
        copy.start()
        sent.append(copy)
        return copy

    with region("wait_v"):
        v_load.wait()
    vt = split(jnp.concatenate([vt_ref[level] for level in order], 0))
    with region("wait_leaf"):
        leaf_load.wait()
    with region("m"):
        high, low = split(leaf[...])
        a_high[:, :lf] = high
        a_low[:, :lf] = low
        for i in range(blocks):
            rows = slice(i * lf, (i + 1) * lf)
            high, low = split(
                dot3([v[:, rows] for v in vt], (a_high[rows, :lf], a_low[rows, :lf]))
            )
            m_high[i] = high
            m_low[i] = low
    with region("wait_u"):
        u_load.wait()
        for copy in core_loads:
            copy.wait()

    def set_local(n, k, gram):
        core = core_l[n][k]
        for ref, top, rest in zip(ch_refs[n], split(core), split(dot(gram, core))):
            ref[k, : 2 * rank] = top
            ref[k, 2 * rank :] = rest

    with region("grams"):
        fast = len(local_levels) == 2 and bits == 3 and 2 * rank == LANES
        if fast:
            ut = {level: split(ut_ref[level]) for level in range(1, levels)}
            rows_v = rank * (levels - 1)
            lane = lax.broadcasted_iota(jnp.int32, (rows_v, LANES), 1) < rank
            tile_a, tile_b = [], []
            for i in range(blocks):
                cols = slice(i * lf, (i + 1) * lf)
                names = [4, 2] if i % 2 == 0 else [2, 4]
                names += [3, 1] if i < 2 else [1, 3]
                rhs = [
                    jnp.concatenate([ut[level][j][:, cols] for level in names], 0)
                    for j in range(2)
                ]
                g = dot3([v[:rows_v, cols] for v in vt], rhs, nt=True)
                tile_a.append(g[:, :LANES])
                tile_b.append(g[:, LANES:])
            s01, s23 = tile_b[0] + tile_b[1], tile_b[2] + tile_b[3]
            even, odd = tile_a[0] + tile_a[2], tile_a[1] + tile_a[3]
            cut = slice(rank, rank * bits)
            gram_out[0] = jnp.where(
                lane[cut], odd[cut] + swap_lanes(even[cut]), s01[cut] + swap_lanes(s23[cut])
            )
        else:
            vr = [v[rank : rank * bits] for v in vt]
            ur = split(jnp.concatenate([ut_ref[level] for level in order], 0))
            gram_out[0] = dot3(vr, [u[:gram_cols] for u in ur], nt=True)
    with region("barrier"):
        pl.semaphore_wait(barrier, bits)
    gram_copy = {0: send(gram_out.at[0], gram_in.at[0], gram_sem.at[0], 0)}
    with region("ch"):
        if fast:
            for k in range(2):
                set_local(1, k, jnp.where(lane, tile_a[2 * k], tile_a[2 * k + 1]))
            cut = slice(0, rank * bits)
            set_local(0, 0, jnp.where(lane[cut], s01[cut], s23[cut]))
        else:
            for n, level in enumerate(local_levels):
                count = 2 ** (level - bits)
                node = rows_dev // count
                half = node // 2
                zero = jnp.zeros((rank, half), BF16)
                own = slice(rank * level, rank * (level + 1))
                for k in range(count):
                    base = k * node
                    diag = [
                        jnp.concatenate(
                            [
                                jnp.concatenate([u[own, base : base + half], zero], 1),
                                jnp.concatenate([zero, u[own, base + half : base + node]], 1),
                            ],
                            0,
                        )
                        for u in ur
                    ]
                    above = [v[: rank * level, base : base + node] for v in vt]
                    set_local(n, k, dot3(above, diag, nt=True))

    first_copy, later_copy, q_copy = {}, {}, {}

    def forward(c):
        right_loads[c].wait()
        high, low = split(rbuf[c])
        r_high[c] = high
        r_low[c] = low
        parts, later = [], []
        for i in range(blocks):
            rows = slice(i * lf, (i + 1) * lf)
            parts.append(dot3((m_high[i], m_low[i]), (r_high[c, rows, :], r_low[c, rows, :])))
        for n in reversed(range(len(local_levels))):
            level = local_levels[n]
            top = rank * level
            merged = []
            for k in range(len(parts) // 2):
                a, b = parts[2 * k], parts[2 * k + 1]
                both = split(jnp.concatenate([b[top:], a[top:]], 0))
                change = dotk([ref[k, 2 * rank :] for ref in ch_refs[n]], both)
                start = local_offset(level, bits, rank) + 2 * rank * k
                later.append((start, n, k, both))
                merged.append(a[:top] + b[:top] - change)
            parts = merged
        p = parts[0]
        low, high = p[:, :LANES], p[:, LANES:]
        first_out[c] = jnp.where(upper, low, high)
        first_copy[c] = send(first_out.at[c], first_in.at[c], first_sem.at[c], 0)
        keep[c] = jnp.where(upper, high, low)
        for start, n, k, both in later:
            ql_ref[c, start : start + 2 * rank] = dotk(
                [ref[k, : 2 * rank] for ref in ch_refs[n]], both
            )

    def bases():
        def turned(rows, width):
            extra = width - rank * len(rows)
            if extra:
                rows = rows + [jnp.zeros((extra, rows_dev), F32)]
            return split(-jnp.concatenate(rows, 0).T)

        if local_levels:
            high, low = turned([ut_ref[level] for level in local_levels], a_high.shape[1] - lf)
            a_high[:, lf:] = high
            a_low[:, lf:] = low
        high, low = turned([ut_ref[bits - 1 - s] for s in range(bits)], u_high.shape[1])
        u_high[...] = high
        u_low[...] = low

    def leaves(c):
        for i in range(blocks):
            rows = slice(i * lf, (i + 1) * lf)
            highs, lows = [r_high[c, rows, :]], [r_low[c, rows, :]]
            width = lf
            for level in local_levels:
                place = rank * (i * 2 ** (level - bits + 1) // blocks)
                start = local_offset(level, bits, rank) + place
                high, low = split(ql_ref[c, start : start + rank])
                highs.append(high)
                lows.append(low)
                width += rank
            if a_high.shape[1] > width:
                zero = jnp.zeros((a_high.shape[1] - width, CHUNK), BF16)
                highs.append(zero)
                lows.append(zero)
            x_ref[c, rows, :] = dotk(
                (a_high[rows, :], a_low[rows, :]),
                (jnp.concatenate(highs, 0), jnp.concatenate(lows, 0)),
            )

    def operator(s):
        core_g_loads[s].wait()
        first = child(s) == 0
        core = core_g[s]
        own = jnp.where(first, core[:rank], core[rank:])
        sib = jnp.where(first, core[rank:], core[:rank])
        parts = [own, sib] if s == 0 else [own]
        if s < bits - 1:
            gram_copy[s].wait_recv()
            rows = slice(rank * s, None)
            if s + 1 < bits - 1:
                gram_out[s + 1] = gram_out[s] + gram_in[s]
                gram_copy[s + 1] = send(
                    gram_out.at[s + 1], gram_in.at[s + 1], gram_sem.at[s + 1], s + 1
                )
            before = [jnp.zeros((rank, 2 * rank), F32)] * s
            after = [jnp.zeros((rank, 2 * rank), F32)] * (gram_cols // rank - 1 - s)
            parts.append(
                -(
                    dot(gram_out[s, rows, :], jnp.concatenate(before + [own] + after, 0))
                    + dot(gram_in[s, rows, :], jnp.concatenate(before + [sib] + after, 0))
                )
            )
        whole = jnp.concatenate(parts, 0)
        high, low = split(jnp.where(first, swap_lanes(whole), whole))
        op_high[s, : high.shape[0]] = high
        op_low[s, : low.shape[0]] = low

    def step(s, c):
        if s == 0:
            first_copy[c].wait_recv()
            mine, theirs = keep[c], first_in[c]
        else:
            later_copy[s, c].wait_recv()
            mine, theirs = later_out[s, c, rank * (s - 1) :], later_in[s, c, rank * (s - 1) :]
        count = rank * (bits - 1 - s) + (2 * rank if s == 0 else rank)
        both = split(jnp.concatenate([mine[:rank], theirs[:rank]], 0))
        image = dotk((op_high[s, :count], op_low[s, :count]), both)
        if s < bits - 1:
            later_out[s + 1, c, rank * s :] = (
                mine[rank:] + theirs[rank:] + image[count - rank * (bits - 1 - s) :]
            )
            part = pl.ds(rank * s, rank * (bits - 1 - s))
            later_copy[s + 1, c] = send(
                later_out.at[s + 1, c, part],
                later_in.at[s + 1, c, part],
                later_sem.at[s, c],
                s + 1,
            )
        q_out[s, c] = image[rank : 2 * rank] if s == 0 else image[:rank]
        q_copy[s, c] = send(
            q_out.at[s, c],
            q_all.at[c, half_id, pl.ds(rank * s, rank)],
            q_sem.at[s, c],
            0,
        )
        q_all[c, half_id, rank * s : rank * (s + 1)] = image[:rank]

    def gathered(c):
        for s in range(bits):
            q_copy[s, c].wait_recv()
        return jnp.concatenate([q_all[c, 0], q_all[c, 1]], 1)

    def apply(c):
        q = gathered(c)
        pad = u_high.shape[1] - q.shape[0]
        if pad:
            q = jnp.concatenate([q, jnp.zeros((pad, CHUNK), F32)], 0)
        x_ref[c] = x_ref[c] + dot3((u_high[...], u_low[...]), split(q))

    for c in range(chunks):
        with region(f"forward{c}"):
            forward(c)
        if c < bits:
            with region(f"operator{c}"):
                operator(c)
    for s in range(chunks, bits):
        operator(s)
    with region("bases"):
        bases()
    for name, *args in schedule(bits, chunks):
        with region(name + "_".join(str(a) for a in args)):
            {"step": step, "leaves": leaves, "apply": apply}[name](*args)
    with region("qwait"):
        q_last[...] = gathered(chunks - 1)
    with region("sent"):
        for copy in sent:
            copy.wait_send()


def tree(bits, right_side, leaf_inverse, vt, ut, cores):
    rows_dev, cols = right_side.shape
    lf = leaf_inverse.shape[1]
    levels, rank = vt.shape[:2]
    blocks = rows_dev // lf
    chunks = cols // CHUNK
    local_levels = list(range(bits, levels))
    assert blocks == 2 ** len(local_levels) and bits >= 2
    gram_cols = pl.cdiv(rank * (bits - 1), LANES) * LANES
    depth = lf + pl.cdiv(rank * len(local_levels), LANES) * LANES
    wide = pl.cdiv(rank * bits, LANES) * LANES
    out_shape = [
        jax.ShapeDtypeStruct((chunks, rows_dev, CHUNK), F32),
        jax.ShapeDtypeStruct((rank * bits, CHUNK), F32),
        jax.ShapeDtypeStruct((rows_dev, wide), BF16),
        jax.ShapeDtypeStruct((rows_dev, wide), BF16),
    ]
    hbm = pl.BlockSpec(memory_space=pltpu.HBM)
    vmem = pl.BlockSpec(memory_space=pltpu.VMEM)
    counts = [2 ** (level - bits) for level in local_levels]
    rest = rank * (bits - 1)
    scratch = [
        pltpu.VMEM((chunks, rows_dev, CHUNK), F32),
        pltpu.VMEM((rows_dev, lf), F32),
        pltpu.VMEM((levels, rank, rows_dev), F32),
        pltpu.VMEM((levels, rank, rows_dev), F32),
        pltpu.VMEM((bits, 2 * rank, 2 * rank), F32),
        pltpu.SemaphoreType.DMA((3 + levels + chunks,)),
        pltpu.VMEM((chunks, rows_dev, CHUNK), BF16),
        pltpu.VMEM((chunks, rows_dev, CHUNK), BF16),
        pltpu.VMEM((rows_dev, depth), BF16),
        pltpu.VMEM((rows_dev, depth), BF16),
        pltpu.VMEM((blocks, levels * rank, lf), BF16),
        pltpu.VMEM((blocks, levels * rank, lf), BF16),
        pltpu.VMEM((chunks, max(rank * (2 * blocks - 2), rank), CHUNK), F32),
        pltpu.VMEM((bits, rank * (bits + 1), 2 * rank), BF16),
        pltpu.VMEM((bits, rank * (bits + 1), 2 * rank), BF16),
        pltpu.VMEM((bits - 1, rest, gram_cols), F32),
        pltpu.VMEM((bits - 1, rest, gram_cols), F32),
        pltpu.VMEM((chunks, rank * bits, LANES), F32),
        pltpu.VMEM((chunks, rank * bits, LANES), F32),
        pltpu.VMEM((chunks, rank * bits, LANES), F32),
        pltpu.VMEM((bits, chunks, rest, LANES), F32),
        pltpu.VMEM((bits, chunks, rest, LANES), F32),
        pltpu.VMEM((bits, chunks, rank, LANES), F32),
        pltpu.VMEM((chunks, 2, rank * bits, LANES), F32),
        pltpu.SemaphoreType.DMA((bits - 1, 2)),
        pltpu.SemaphoreType.DMA((chunks, 2)),
        pltpu.SemaphoreType.DMA((bits - 1, chunks, 2)),
        pltpu.SemaphoreType.DMA((bits, chunks, 2)),
    ]
    scratch += [pltpu.VMEM((count, 2 * rank, 2 * rank), F32) for count in counts]
    scratch += [
        pltpu.VMEM((count, rank * (level + 2), 2 * rank), BF16)
        for count, level in zip(counts, local_levels)
        for _ in range(2)
    ]
    return pl.pallas_call(
        functools.partial(tree_kernel, bits, levels, blocks),
        out_shape=out_shape,
        in_specs=[hbm] * 5,
        out_specs=[vmem] * 4,
        scratch_shapes=scratch,
        compiler_params=pltpu.CompilerParams(
            collective_id=0, has_side_effects=True, vmem_limit_bytes=TREE_VMEM + 32 * rows_dev * lf
        ),
        name="tree",
    )(right_side, leaf_inverse, vt, ut, cores)


def finish_kernel(x_ref, q_ref, uh_ref, ul_ref, out_hbm, last, sems):
    chunks, rows_dev, width = x_ref.shape
    copies = []

    def write(src, rows, c):
        dst = out_hbm.at[pl.ds(rows, src.shape[0]), pl.ds(c * width, width)]
        copy = pltpu.make_async_copy(src, dst, sems.at[len(copies)])
        copy.start()
        copies.append(copy)

    for c in range(chunks - 1):
        write(x_ref.at[c], 0, c)
    q = q_ref[...]
    pad = uh_ref.shape[1] - q.shape[0]
    if pad:
        q = jnp.concatenate([q, jnp.zeros((pad, width), F32)], 0)
    q = split(q)
    piece = rows_dev // (sems.shape[0] - (chunks - 1))
    for start in range(0, rows_dev, piece):
        rows = slice(start, start + piece)
        last[rows] = x_ref[chunks - 1, rows] + dot3((uh_ref[rows], ul_ref[rows]), q)
        write(last.at[pl.ds(start, piece)], start, chunks - 1)
    for copy in copies:
        copy.wait()


def finish(x, q, u_high, u_low):
    chunks, rows_dev, width = x.shape
    vmem = pl.BlockSpec(memory_space=pltpu.VMEM)
    return pl.pallas_call(
        finish_kernel,
        out_shape=jax.ShapeDtypeStruct((rows_dev, chunks * width), F32),
        in_specs=[vmem] * 4,
        out_specs=pl.BlockSpec(memory_space=pltpu.HBM),
        scratch_shapes=[
            pltpu.VMEM((rows_dev, width), F32),
            pltpu.SemaphoreType.DMA((chunks - 1 + 4,)),
        ],
        compiler_params=pltpu.CompilerParams(vmem_limit_bytes=FINISH_VMEM),
        name="finish",
    )(x, q, u_high, u_low)


def local(bits, right_side, leaf_inverse, left_factors, right_factors, cores):
    ut = jnp.swapaxes(left_factors, 1, 2)
    vt = jnp.swapaxes(right_factors, 1, 2)
    right_side, leaf_inverse, vt, ut, cores = (
        pltpu.with_memory_space_constraint(a, pltpu.HBM)
        for a in (right_side, leaf_inverse, vt, ut, cores)
    )
    return finish(*tree(bits, right_side, leaf_inverse, vt, ut, cores))


def solution(mesh):
    bits = mesh.shape["rows"].bit_length() - 1
    in_specs = (
        P(("rep", "rows"), None),
        P(("rep", "rows"), None),
        P(None, ("rep", "rows"), None),
        P(None, ("rep", "rows"), None),
        P("rep", None, None),
    )
    out_specs = P(("rep", "rows"), None)
    return jax.shard_map(
        functools.partial(local, bits),
        mesh=mesh,
        in_specs=in_specs,
        out_specs=out_specs,
        check_vma=False,
    )
```

time: 37.6 us -> 35.8 us (0.952)
  Pallas kernels: 37.5 us -> 35.6 us
    pallas_call x1, Pallas kernels: 3.99 us -> 2.08 us  [finish(): pl.pallas_call(finish_kernel, out_shape=jax.ShapeDtypeStruct((rows_dev, c...]
where the time goes in v1:
time: 35.8 us; the launch traced here: 35.6 us
  Pallas kernels  35.6 us (99%)
    pallas_call x1, Pallas kernels, tree(): pl.pallas_call(functools.partial(tree_kernel, bits, levels, blocks), out_...  33.5 us
    pallas_call x1, Pallas kernels, finish(): pl.pallas_call(finish_kernel, out_shape=jax.ShapeDtypeStruct((rows_dev, c...  2.08 us

profile of v1, /device:TPU:0, one launch (start us, length us, event | category | flops | bytes accessed | tf_op | source)
XLA Modules:
  0.0 35.6 jit_solution(6172979496210287507)
XLA Ops:
  0.0 33.5 %tree.1 = (f32[4,1024,256]{2,1,0:T(8,128)S(1)}, f32[192,256]{1,0:T(8,128)S(1)}, bf16[1024,256]{1,0:T(8,128)(2,1)S(1)}, bf16[1024,256]{1,0:T(8,128)(2,1)S(1)}) custom-call(f32[1024,1024]{1,0:T(8,128)} %right_hbm.1, f32[1024,256]{1,0:T(8,128)} %leaf_hbm.1, f32[5,64,1024]{2,1,0:T(8,128)} %bitcast.2, f32[5,64,1024]{2,1,0:T(8,128)} %bitcast.3, ...), custom_call_target="tpu_custom_call" | custom-call | tf_op jit(solution)/shard_map/tree/pallas_call | solution.py:455
  33.5 2.1 %finish.1 = f32[1024,1024]{1,0:T(8,128)} custom-call(f32[4,1024,256]{2,1,0:T(8,128)S(1)} %get-tuple-element.9.x_ref, f32[192,256]{1,0:T(8,128)S(1)} %get-tuple-element.10.q_ref, bf16[1024,256]{1,0:T(8,128)(2,1)S(1)} %get-tuple-element.11.uh_ref, bf16[1024,256]{1,0:T(8,128)(2,1)S(1)} %get-tuple-element.12.ul_ref), custom_call_target="tpu_custom_call" | custom-call | tf_op jit(solution)/shard_map/finish/pallas_call | solution.py:497

commit v2 on v1

--- a/solution.py
+++ b/solution.py
@@ -16,6 +16,9 @@
 FINISH_VMEM = 12 << 20
 MESH = pl.DeviceIdType.MESH
 TRACE = False
+LATE = 2
+PIECES = 2
+CROSS = True
 
 
 def region(name):
@@ -62,32 +65,44 @@
 def schedule(bits, chunks):
     if bits == 3 and chunks == 4:
         return [
-            ("step", 0, 0), ("leaves", 0), ("step", 0, 1), ("leaves", 1),
-            ("step", 1, 0), ("step", 0, 2), ("leaves", 2), ("step", 1, 1),
-            ("step", 0, 3), ("step", 2, 0), ("step", 1, 2), ("leaves", 3),
-            ("step", 2, 1), ("step", 1, 3), ("apply", 0), ("step", 2, 2),
-            ("apply", 1), ("step", 2, 3), ("apply", 2),
+            (None, "forward", 0), (None, "forward", 1), (None, "operator", 0),
+            (None, "forward", 2), (None, "step", 0, 0), (None, "forward", 3),
+            (None, "give", 0, 0), (None, "step", 0, 1), (None, "bases"), (None, "operator", 1),
+            (None, "step", 1, 0), (None, "give", 1, 0), (None, "step", 0, 2),
+            (False, "leaves", 2), (None, "give", 0, 1), (None, "give", 0, 2),
+            (None, "step", 1, 1), (False, "leaves", 0), (None, "step", 0, 3),
+            (None, "operator", 2), (None, "step", 2, 0), (None, "give", 2, 0),
+            (None, "give", 1, 1), (None, "step", 1, 2), (True, "leaves", 2), (None, "leaves", 1),
+            (True, "leaves", 3), (True, "leaves", 0), (None, "give", 1, 2), (None, "step", 1, 3),
+            (None, "step", 2, 1), (True, "apply", 0), (None, "give", 2, 1), (False, "leaves", 3),
+            (None, "step", 2, 2), (None, "give", 1, 3), (None, "give", 0, 3),
+            (None, "give", 2, 2), (False, "apply", 0), (None, "apply", 1), (None, "step", 2, 3),
         ]
-    order = []
+    order = [("forward", c) for c in range(chunks)]
+    order += [("operator", s) for s in range(bits)] + [("bases",)]
     for t in range(chunks + bits - 1):
         for s in range(bits):
             if 0 <= t - s < chunks:
                 order.append(("step", s, t - s))
+                if not (CROSS and s == bits - 1 and t - s == chunks - 1):
+                    order.append(("give", s, t - s))
         if t < chunks:
             order.append(("leaves", t))
-    return order + [("apply", c) for c in range(chunks - 1)]
+    order += [("apply", c) for c in range(chunks - LATE)]
+    return [(None, *item) for item in order]
 
 
 def tree_kernel(bits, levels, blocks, right_hbm, leaf_hbm, vt_hbm, ut_hbm, cores_hbm, *refs):
-    x_ref, q_last, u_high, u_low = refs[:4]
+    x_ref, q_late, u_high, u_low = refs[:4]
     rbuf, leaf, vt_ref, ut_ref, core_g, sem_in = refs[4:10]
     r_high, r_low, a_high, a_low, m_high, m_low, ql_ref = refs[10:17]
     op_high, op_low, gram_out, gram_in, keep, first_out, first_in = refs[17:24]
     later_out, later_in, q_out, q_all = refs[24:28]
     gram_sem, first_sem, later_sem, q_sem = refs[28:32]
+    last_in, last_sem = refs[32:34]
     local_levels = list(range(bits, levels))
-    core_l = refs[32 : 32 + len(local_levels)]
-    ch_refs = refs[32 + len(local_levels) :]
+    core_l = refs[34 : 34 + len(local_levels)]
+    ch_refs = refs[34 + len(local_levels) :]
     ch_refs = list(zip(ch_refs[::2], ch_refs[1::2]))
 
     me = lax.axis_index("rows")
@@ -98,6 +113,7 @@
     upper = half_id == 1
     order = level_order(bits, levels)
     gram_cols = gram_out.shape[2]
+    second = lax.rem(lax.axis_index("rep"), 2) == 1
 
     def child(s):
         return lax.rem(me // 2**s, 2)
@@ -105,11 +121,11 @@
     def partner(s):
         return me + (1 - 2 * child(s)) * 2**s
 
+    cross = partner(bits - 1) + (1 - 2 * child(0))
+    greeted = [partner(s) for s in range(bits)] + ([cross] if CROSS else [])
     barrier = pltpu.get_barrier_semaphore()
-    for s in range(bits):
-        pl.semaphore_signal(
-            barrier, inc=1, device_id={"rows": partner(s)}, device_id_type=MESH
-        )
+    for target in greeted:
+        pl.semaphore_signal(barrier, inc=1, device_id={"rows": target}, device_id_type=MESH)
 
     slots = [0]
 
@@ -137,13 +153,13 @@
 
     sent = []
 
-    def send(src, dst, sems, s):
+    def send(src, dst, sems, target):
         copy = pltpu.make_async_remote_copy(
             src_ref=src,
             dst_ref=dst,
             send_sem=sems.at[0],
             recv_sem=sems.at[1],
-            device_id={"rows": partner(s)},
+            device_id={"rows": target},
             device_id_type=MESH,
         )
         copy.start()
@@ -206,8 +222,8 @@
             ur = split(jnp.concatenate([ut_ref[level] for level in order], 0))
             gram_out[0] = dot3(vr, [u[:gram_cols] for u in ur], nt=True)
     with region("barrier"):
-        pl.semaphore_wait(barrier, bits)
-    gram_copy = {0: send(gram_out.at[0], gram_in.at[0], gram_sem.at[0], 0)}
+        pl.semaphore_wait(barrier, len(greeted))
+    gram_copy = {0: send(gram_out.at[0], gram_in.at[0], gram_sem.at[0], partner(0))}
     with region("ch"):
         if fast:
             for k in range(2):
@@ -236,7 +252,7 @@
                     above = [v[: rank * level, base : base + node] for v in vt]
                     set_local(n, k, dot3(above, diag, nt=True))
 
-    first_copy, later_copy, q_copy = {}, {}, {}
+    first_copy, later_copy, q_copy, last_copy = {}, {}, {}, []
 
     def forward(c):
         right_loads[c].wait()
@@ -262,7 +278,7 @@
         p = parts[0]
         low, high = p[:, :LANES], p[:, LANES:]
         first_out[c] = jnp.where(upper, low, high)
-        first_copy[c] = send(first_out.at[c], first_in.at[c], first_sem.at[c], 0)
+        first_copy[c] = send(first_out.at[c], first_in.at[c], first_sem.at[c], partner(0))
         keep[c] = jnp.where(upper, high, low)
         for start, n, k, both in later:
             ql_ref[c, start : start + 2 * rank] = dotk(
@@ -318,7 +334,10 @@
             if s + 1 < bits - 1:
                 gram_out[s + 1] = gram_out[s] + gram_in[s]
                 gram_copy[s + 1] = send(
-                    gram_out.at[s + 1], gram_in.at[s + 1], gram_sem.at[s + 1], s + 1
+                    gram_out.at[s + 1],
+                    gram_in.at[s + 1],
+                    gram_sem.at[s + 1],
+                    partner(s + 1),
                 )
             before = [jnp.zeros((rank, 2 * rank), F32)] * s
             after = [jnp.zeros((rank, 2 * rank), F32)] * (gram_cols // rank - 1 - s)
@@ -333,6 +352,18 @@
         op_high[s, : high.shape[0]] = high
         op_low[s, : low.shape[0]] = low
 
+    def crossed(s, c):
+        return CROSS and s == bits - 1 and c == chunks - 1
+
+    def halves(c, rows, value):
+        q_all[c, 0, rows] = value[:, :LANES]
+        q_all[c, 1, rows] = value[:, LANES:]
+
+    def join(here, there):
+        return jnp.concatenate(
+            [jnp.where(upper, there, here), jnp.where(upper, here, there)], 1
+        )
+
     def step(s, c):
         if s == 0:
             first_copy[c].wait_recv()
@@ -340,9 +371,17 @@
         else:
             later_copy[s, c].wait_recv()
             mine, theirs = later_out[s, c, rank * (s - 1) :], later_in[s, c, rank * (s - 1) :]
+        if crossed(s, c):
+            for copy in last_copy:
+                copy.wait_recv()
+            mine, theirs = join(mine, last_in[0]), join(theirs, last_in[1])
         count = rank * (bits - 1 - s) + (2 * rank if s == 0 else rank)
         both = split(jnp.concatenate([mine[:rank], theirs[:rank]], 0))
         image = dotk((op_high[s, :count], op_low[s, :count]), both)
+        own = slice(rank * s, rank * (s + 1))
+        if crossed(s, c):
+            halves(c, own, image)
+            return
         if s < bits - 1:
             later_out[s + 1, c, rank * s :] = (
                 mine[rank:] + theirs[rank:] + image[count - rank * (bits - 1 - s) :]
@@ -352,20 +391,27 @@
                 later_out.at[s + 1, c, part],
                 later_in.at[s + 1, c, part],
                 later_sem.at[s, c],
-                s + 1,
-            )
+                partner(s + 1),
+            )
+            if crossed(s + 1, c):
+                root = later_out.at[s + 1, c, pl.ds(rank * s, rank)]
+                last_copy.append(send(root, last_in.at[1], last_sem.at[1], cross))
+                last_copy.append(send(root, last_in.at[0], last_sem.at[0], partner(0)))
         q_out[s, c] = image[rank : 2 * rank] if s == 0 else image[:rank]
+        q_all[c, half_id, own] = image[:rank]
+
+    def give(s, c):
         q_copy[s, c] = send(
             q_out.at[s, c],
             q_all.at[c, half_id, pl.ds(rank * s, rank)],
             q_sem.at[s, c],
-            0,
+            partner(0),
         )
-        q_all[c, half_id, rank * s : rank * (s + 1)] = image[:rank]
 
     def gathered(c):
         for s in range(bits):
-            q_copy[s, c].wait_recv()
+            if not crossed(s, c):
+                q_copy[s, c].wait_recv()
         return jnp.concatenate([q_all[c, 0], q_all[c, 1]], 1)
 
     def apply(c):
@@ -375,21 +421,16 @@
             q = jnp.concatenate([q, jnp.zeros((pad, CHUNK), F32)], 0)
         x_ref[c] = x_ref[c] + dot3((u_high[...], u_low[...]), split(q))
 
-    for c in range(chunks):
-        with region(f"forward{c}"):
-            forward(c)
-        if c < bits:
-            with region(f"operator{c}"):
-                operator(c)
-    for s in range(chunks, bits):
-        operator(s)
-    with region("bases"):
-        bases()
-    for name, *args in schedule(bits, chunks):
+    parts = {f.__name__: f for f in (forward, operator, bases, step, give, leaves, apply)}
+    for where, name, *args in schedule(bits, chunks):
         with region(name + "_".join(str(a) for a in args)):
-            {"step": step, "leaves": leaves, "apply": apply}[name](*args)
+            if where is None:
+                parts[name](*args)
+            else:
+                pl.when(second == where)(functools.partial(parts[name], *args))
     with region("qwait"):
-        q_last[...] = gathered(chunks - 1)
+        for c in range(chunks - LATE, chunks):
+            q_late[c - chunks + LATE] = gathered(c)
     with region("sent"):
         for copy in sent:
             copy.wait_send()
@@ -408,7 +449,7 @@
     wide = pl.cdiv(rank * bits, LANES) * LANES
     out_shape = [
         jax.ShapeDtypeStruct((chunks, rows_dev, CHUNK), F32),
-        jax.ShapeDtypeStruct((rank * bits, CHUNK), F32),
+        jax.ShapeDtypeStruct((LATE, rank * bits, CHUNK), F32),
         jax.ShapeDtypeStruct((rows_dev, wide), BF16),
         jax.ShapeDtypeStruct((rows_dev, wide), BF16),
     ]
@@ -445,6 +486,8 @@
         pltpu.SemaphoreType.DMA((chunks, 2)),
         pltpu.SemaphoreType.DMA((bits - 1, chunks, 2)),
         pltpu.SemaphoreType.DMA((bits, chunks, 2)),
+        pltpu.VMEM((2, rank, LANES), F32),
+        pltpu.SemaphoreType.DMA((2, 2)),
     ]
     scratch += [pltpu.VMEM((count, 2 * rank, 2 * rank), F32) for count in counts]
     scratch += [
@@ -475,18 +518,21 @@
         copy.start()
         copies.append(copy)
 
-    for c in range(chunks - 1):
+    late = q_ref.shape[0]
+    for c in range(chunks - late):
         write(x_ref.at[c], 0, c)
-    q = q_ref[...]
-    pad = uh_ref.shape[1] - q.shape[0]
-    if pad:
-        q = jnp.concatenate([q, jnp.zeros((pad, width), F32)], 0)
-    q = split(q)
-    piece = rows_dev // (sems.shape[0] - (chunks - 1))
-    for start in range(0, rows_dev, piece):
-        rows = slice(start, start + piece)
-        last[rows] = x_ref[chunks - 1, rows] + dot3((uh_ref[rows], ul_ref[rows]), q)
-        write(last.at[pl.ds(start, piece)], start, chunks - 1)
+    piece = rows_dev // PIECES
+    for n in range(late):
+        q = q_ref[n]
+        pad = uh_ref.shape[1] - q.shape[0]
+        if pad:
+            q = jnp.concatenate([q, jnp.zeros((pad, width), F32)], 0)
+        q = split(q)
+        c = chunks - late + n
+        for start in range(0, rows_dev, piece):
+            rows = slice(start, start + piece)
+            last[n, rows] = x_ref[c, rows] + dot3((uh_ref[rows], ul_ref[rows]), q)
+            write(last.at[n, pl.ds(start, piece)], start, c)
     for copy in copies:
         copy.wait()
 
@@ -500,8 +546,8 @@
         in_specs=[vmem] * 4,
         out_specs=pl.BlockSpec(memory_space=pltpu.HBM),
         scratch_shapes=[
-            pltpu.VMEM((rows_dev, width), F32),
-            pltpu.SemaphoreType.DMA((chunks - 1 + 4,)),
+            pltpu.VMEM((q.shape[0], rows_dev, width), F32),
+            pltpu.SemaphoreType.DMA((chunks + q.shape[0] * (PIECES - 1),)),
         ],
         compiler_params=pltpu.CompilerParams(vmem_limit_bytes=FINISH_VMEM),
         name="finish",

time: 35.8 us -> 31.5 us (0.88)
  Pallas kernels: 35.6 us -> 31.3 us
    pallas_call x1, Pallas kernels: 33.5 us -> 29.2 us  [tree(): pl.pallas_call(functools.partial(tree_kernel, bits, levels, blocks), out_...]
where the time goes in v2:
time: 31.5 us; the launch traced here: 31.3 us
  Pallas kernels  31.3 us (99%)
    pallas_call x1, Pallas kernels, tree(): pl.pallas_call(functools.partial(tree_kernel, bits, levels, blocks), out_...  29.2 us
    pallas_call x1, Pallas kernels, finish(): pl.pallas_call(finish_kernel, out_shape=jax.ShapeDtypeStruct((rows_dev, c...  2.09 us

profile of v2, /device:TPU:0, one launch (start us, length us, event | category | flops | bytes accessed | tf_op | source)
XLA Modules:
  0.0 31.3 jit_solution(18102640117181610431)
XLA Ops:
  0.0 29.2 %tree.1 = (f32[4,1024,256]{2,1,0:T(8,128)S(1)}, f32[2,192,256]{2,1,0:T(8,128)S(1)}, bf16[1024,256]{1,0:T(8,128)(2,1)S(1)}, bf16[1024,256]{1,0:T(8,128)(2,1)S(1)}) custom-call(f32[1024,1024]{1,0:T(8,128)} %right_hbm.1, f32[1024,256]{1,0:T(8,128)} %leaf_hbm.1, f32[5,64,1024]{2,1,0:T(8,128)} %bitcast.2, f32[5,64,1024]{2,1,0:T(8,128)} %bitcast.3, ...), custom_call_target="tpu_custom_call" | custom-call | tf_op jit(solution)/shard_map/tree/pallas_call | solution.py:498
  29.3 2.1 %finish.1 = f32[1024,1024]{1,0:T(8,128)} custom-call(f32[4,1024,256]{2,1,0:T(8,128)S(1)} %get-tuple-element.9.x_ref, f32[2,192,256]{2,1,0:T(8,128)S(1)} %get-tuple-element.10.q_ref, bf16[1024,256]{1,0:T(8,128)(2,1)S(1)} %get-tuple-element.11.uh_ref, bf16[1024,256]{1,0:T(8,128)(2,1)S(1)} %get-tuple-element.12.ul_ref), custom_call_target="tpu_custom_call" | custom-call | tf_op jit(solution)/shard_map/finish/pallas_call | solution.py:543

commit v3 on v2

--- a/solution.py
+++ b/solution.py
@@ -99,10 +99,10 @@
     op_high, op_low, gram_out, gram_in, keep, first_out, first_in = refs[17:24]
     later_out, later_in, q_out, q_all = refs[24:28]
     gram_sem, first_sem, later_sem, q_sem = refs[28:32]
-    last_in, last_sem = refs[32:34]
+    last_in, last_sem, send_sem = refs[32:35]
     local_levels = list(range(bits, levels))
-    core_l = refs[34 : 34 + len(local_levels)]
-    ch_refs = refs[34 + len(local_levels) :]
+    core_l = refs[35 : 35 + len(local_levels)]
+    ch_refs = refs[35 + len(local_levels) :]
     ch_refs = list(zip(ch_refs[::2], ch_refs[1::2]))
 
     me = lax.axis_index("rows")
@@ -122,7 +122,7 @@
         return me + (1 - 2 * child(s)) * 2**s
 
     cross = partner(bits - 1) + (1 - 2 * child(0))
-    greeted = [partner(s) for s in range(bits)] + ([cross] if CROSS else [])
+    greeted = [partner(s) for s in range(bits)]
     barrier = pltpu.get_barrier_semaphore()
     for target in greeted:
         pl.semaphore_signal(barrier, inc=1, device_id={"rows": target}, device_id_type=MESH)
@@ -146,24 +146,24 @@
     right_loads = [
         load(right_hbm.at[:, pl.ds(c * CHUNK, CHUNK)], rbuf.at[c]) for c in range(chunks)
     ]
-    core_g_loads = []
     for s in range(bits):
         src = cores_hbm.at[2 ** (bits - 1 - s) - 1 + me // 2 ** (s + 1)]
-        core_g_loads.append(load(src, core_g.at[s]))
+        pltpu.make_async_copy(src, core_g.at[s], sem_in.at[slots[0]]).start()
+    core_g_load = pltpu.make_async_copy(core_g, core_g, sem_in.at[slots[0]])
 
     sent = []
 
-    def send(src, dst, sems, target):
+    def send(src, dst, sem, target):
         copy = pltpu.make_async_remote_copy(
             src_ref=src,
             dst_ref=dst,
-            send_sem=sems.at[0],
-            recv_sem=sems.at[1],
+            send_sem=send_sem.at[0],
+            recv_sem=sem,
             device_id={"rows": target},
             device_id_type=MESH,
         )
         copy.start()
-        sent.append(copy)
+        sent.append(src.shape[0] * src.shape[1])
         return copy
 
     with region("wait_v"):
@@ -252,7 +252,7 @@
                     above = [v[: rank * level, base : base + node] for v in vt]
                     set_local(n, k, dot3(above, diag, nt=True))
 
-    first_copy, later_copy, q_copy, last_copy = {}, {}, {}, []
+    first_copy, later_copy, last_copy = {}, {}, []
 
     def forward(c):
         right_loads[c].wait()
@@ -322,7 +322,8 @@
             )
 
     def operator(s):
-        core_g_loads[s].wait()
+        if s == 0:
+            core_g_load.wait()
         first = child(s) == 0
         core = core_g[s]
         own = jnp.where(first, core[:rank], core[rank:])
@@ -401,17 +402,12 @@
         q_all[c, half_id, own] = image[:rank]
 
     def give(s, c):
-        q_copy[s, c] = send(
-            q_out.at[s, c],
-            q_all.at[c, half_id, pl.ds(rank * s, rank)],
-            q_sem.at[s, c],
-            partner(0),
-        )
+        place = q_all.at[c, half_id, pl.ds(rank * s, rank)]
+        send(q_out.at[s, c], place, q_sem.at[c], partner(0))
 
     def gathered(c):
-        for s in range(bits):
-            if not crossed(s, c):
-                q_copy[s, c].wait_recv()
+        given = q_all.at[c, 0, pl.ds(0, rank * (bits - 1 if crossed(bits - 1, c) else bits))]
+        pltpu.make_async_copy(given, given, q_sem.at[c]).wait()
         return jnp.concatenate([q_all[c, 0], q_all[c, 1]], 1)
 
     def apply(c):
@@ -432,8 +428,10 @@
         for c in range(chunks - LATE, chunks):
             q_late[c - chunks + LATE] = gathered(c)
     with region("sent"):
-        for copy in sent:
-            copy.wait_send()
+        rows = sum(sent) // (chunks * CHUNK)
+        assert rows * chunks * CHUNK == sum(sent) and rows <= rows_dev
+        everything = rbuf.at[:, pl.ds(0, rows)]
+        pltpu.make_async_copy(everything, everything, send_sem.at[0]).wait()
 
 
 def tree(bits, right_side, leaf_inverse, vt, ut, cores):
@@ -463,7 +461,7 @@
         pltpu.VMEM((levels, rank, rows_dev), F32),
         pltpu.VMEM((levels, rank, rows_dev), F32),
         pltpu.VMEM((bits, 2 * rank, 2 * rank), F32),
-        pltpu.SemaphoreType.DMA((3 + levels + chunks,)),
+        pltpu.SemaphoreType.DMA((4 + len(local_levels) + chunks,)),
         pltpu.VMEM((chunks, rows_dev, CHUNK), BF16),
         pltpu.VMEM((chunks, rows_dev, CHUNK), BF16),
         pltpu.VMEM((rows_dev, depth), BF16),
@@ -482,12 +480,13 @@
         pltpu.VMEM((bits, chunks, rest, LANES), F32),
         pltpu.VMEM((bits, chunks, rank, LANES), F32),
         pltpu.VMEM((chunks, 2, rank * bits, LANES), F32),
-        pltpu.SemaphoreType.DMA((bits - 1, 2)),
-        pltpu.SemaphoreType.DMA((chunks, 2)),
-        pltpu.SemaphoreType.DMA((bits - 1, chunks, 2)),
-        pltpu.SemaphoreType.DMA((bits, chunks, 2)),
+        pltpu.SemaphoreType.DMA((bits - 1,)),
+        pltpu.SemaphoreType.DMA((chunks,)),
+        pltpu.SemaphoreType.DMA((bits - 1, chunks)),
+        pltpu.SemaphoreType.DMA((chunks,)),
         pltpu.VMEM((2, rank, LANES), F32),
-        pltpu.SemaphoreType.DMA((2, 2)),
+        pltpu.SemaphoreType.DMA((2,)),
+        pltpu.SemaphoreType.DMA((1,)),
     ]
     scratch += [pltpu.VMEM((count, 2 * rank, 2 * rank), F32) for count in counts]
     scratch += [

time: 31.5 us -> 31 us (0.984)
  Pallas kernels: 31.3 us -> 30.8 us
    pallas_call x1, Pallas kernels: 29.2 us -> 28.7 us  [tree(): pl.pallas_call(functools.partial(tree_kernel, bits, levels, blocks), out_...]
where the time goes in v3:
time: 31 us; the launch traced here: 30.8 us
  Pallas kernels  30.8 us (99%)
    pallas_call x1, Pallas kernels, tree(): pl.pallas_call(functools.partial(tree_kernel, bits, levels, blocks), out_...  28.7 us
    pallas_call x1, Pallas kernels, finish(): pl.pallas_call(finish_kernel, out_shape=jax.ShapeDtypeStruct((rows_dev, c...  2.09 us

profile of v3, /device:TPU:0, one launch (start us, length us, event | category | flops | bytes accessed | tf_op | source)
XLA Modules:
  0.0 30.8 jit_solution(14696420255068805879)
XLA Ops:
  0.0 28.7 %tree.1 = (f32[4,1024,256]{2,1,0:T(8,128)S(1)}, f32[2,192,256]{2,1,0:T(8,128)S(1)}, bf16[1024,256]{1,0:T(8,128)(2,1)S(1)}, bf16[1024,256]{1,0:T(8,128)(2,1)S(1)}) custom-call(f32[1024,1024]{1,0:T(8,128)} %right_hbm.1, f32[1024,256]{1,0:T(8,128)} %leaf_hbm.1, f32[5,64,1024]{2,1,0:T(8,128)} %bitcast.2, f32[5,64,1024]{2,1,0:T(8,128)} %bitcast.3, ...), custom_call_target="tpu_custom_call" | custom-call | tf_op jit(solution)/shard_map/tree/pallas_call | solution.py:497
  28.7 2.1 %finish.1 = f32[1024,1024]{1,0:T(8,128)} custom-call(f32[4,1024,256]{2,1,0:T(8,128)S(1)} %get-tuple-element.9.x_ref, f32[2,192,256]{2,1,0:T(8,128)S(1)} %get-tuple-element.10.q_ref, bf16[1024,256]{1,0:T(8,128)(2,1)S(1)} %get-tuple-element.11.uh_ref, bf16[1024,256]{1,0:T(8,128)(2,1)S(1)} %get-tuple-element.12.ul_ref), custom_call_target="tpu_custom_call" | custom-call | tf_op jit(solution)/shard_map/finish/pallas_call | solution.py:542

commit v4 on v3

--- a/solution.py
+++ b/solution.py
@@ -65,18 +65,18 @@
 def schedule(bits, chunks):
     if bits == 3 and chunks == 4:
         return [
-            (None, "forward", 0), (None, "forward", 1), (None, "operator", 0),
-            (None, "forward", 2), (None, "step", 0, 0), (None, "forward", 3),
-            (None, "give", 0, 0), (None, "step", 0, 1), (None, "bases"), (None, "operator", 1),
-            (None, "step", 1, 0), (None, "give", 1, 0), (None, "step", 0, 2),
-            (False, "leaves", 2), (None, "give", 0, 1), (None, "give", 0, 2),
-            (None, "step", 1, 1), (False, "leaves", 0), (None, "step", 0, 3),
-            (None, "operator", 2), (None, "step", 2, 0), (None, "give", 2, 0),
-            (None, "give", 1, 1), (None, "step", 1, 2), (True, "leaves", 2), (None, "leaves", 1),
-            (True, "leaves", 3), (True, "leaves", 0), (None, "give", 1, 2), (None, "step", 1, 3),
-            (None, "step", 2, 1), (True, "apply", 0), (None, "give", 2, 1), (False, "leaves", 3),
-            (None, "step", 2, 2), (None, "give", 1, 3), (None, "give", 0, 3),
-            (None, "give", 2, 2), (False, "apply", 0), (None, "apply", 1), (None, "step", 2, 3),
+            (None, "forward", 0), (True, "bases"), (None, "forward", 1), (None, "operator", 0),
+            (True, "leaves", 0), (None, "forward", 2), (None, "step", 0, 0), (None, "forward", 3),
+            (None, "step", 0, 1), (None, "operator", 1), (False, "bases"), (None, "step", 1, 0),
+            (None, "step", 0, 2), (False, "leaves", 3), (None, "step", 0, 3),
+            (None, "give", 0, 0), (None, "give", 1, 0), (None, "give", 0, 1),
+            (None, "step", 1, 1), (True, "leaves", 3), (False, "leaves", 2), (None, "give", 0, 2),
+            (None, "give", 0, 3), (None, "give", 1, 1), (None, "operator", 2),
+            (None, "step", 1, 2), (None, "give", 1, 2), (None, "step", 2, 0),
+            (None, "give", 2, 0), (True, "leaves", 2), (False, "leaves", 1), (None, "step", 1, 3),
+            (True, "leaves", 1), (False, "leaves", 0), (None, "step", 2, 1), (None, "give", 1, 3),
+            (None, "give", 2, 1), ("early", "apply", 0), (None, "step", 2, 2),
+            (None, "give", 2, 2), ("late", "apply", 0), (None, "apply", 1), (None, "step", 2, 3),
         ]
     order = [("forward", c) for c in range(chunks)]
     order += [("operator", s) for s in range(bits)] + [("bases",)]
@@ -95,14 +95,14 @@
 def tree_kernel(bits, levels, blocks, right_hbm, leaf_hbm, vt_hbm, ut_hbm, cores_hbm, *refs):
     x_ref, q_late, u_high, u_low = refs[:4]
     rbuf, leaf, vt_ref, ut_ref, core_g, sem_in = refs[4:10]
-    r_high, r_low, a_high, a_low, m_high, m_low, ql_ref = refs[10:17]
-    op_high, op_low, gram_out, gram_in, keep, first_out, first_in = refs[17:24]
-    later_out, later_in, q_out, q_all = refs[24:28]
-    gram_sem, first_sem, later_sem, q_sem = refs[28:32]
-    last_in, last_sem, send_sem = refs[32:35]
+    r_high, r_low, a_high, a_low, m_high, m_low, *both_refs = refs[10:18]
+    op_high, op_low, gram_out, gram_in, keep, first_out, first_in = refs[18:25]
+    later_out, later_in, q_out, q_all = refs[25:29]
+    gram_sem, first_sem, later_sem, q_sem = refs[29:33]
+    last_in, last_sem, send_sem = refs[33:36]
     local_levels = list(range(bits, levels))
-    core_l = refs[35 : 35 + len(local_levels)]
-    ch_refs = refs[35 + len(local_levels) :]
+    core_l = refs[36 : 36 + len(local_levels)]
+    ch_refs = refs[36 + len(local_levels) :]
     ch_refs = list(zip(ch_refs[::2], ch_refs[1::2]))
 
     me = lax.axis_index("rows")
@@ -135,8 +135,13 @@
         copy.start()
         return copy
 
-    v_load = load(vt_hbm, vt_ref)
-    leaf_load = load(leaf_hbm, leaf)
+    pieces = 2 if blocks % 2 == 0 else 1
+    width = rows_dev // pieces
+    v_loads, leaf_loads = [], []
+    for n in range(pieces):
+        part = pl.ds(n * width, width)
+        v_loads.append(load(vt_hbm.at[:, :, part], vt_ref.at[:, :, part]))
+        leaf_loads.append(load(leaf_hbm.at[part], leaf.at[part]))
     u_load = load(ut_hbm, ut_ref)
     core_loads = []
     for n, level in enumerate(local_levels):
@@ -166,22 +171,26 @@
         sent.append(src.shape[0] * src.shape[1])
         return copy
 
-    with region("wait_v"):
-        v_load.wait()
-    vt = split(jnp.concatenate([vt_ref[level] for level in order], 0))
-    with region("wait_leaf"):
-        leaf_load.wait()
-    with region("m"):
-        high, low = split(leaf[...])
-        a_high[:, :lf] = high
-        a_low[:, :lf] = low
-        for i in range(blocks):
-            rows = slice(i * lf, (i + 1) * lf)
-            high, low = split(
-                dot3([v[:, rows] for v in vt], (a_high[rows, :lf], a_low[rows, :lf]))
-            )
-            m_high[i] = high
-            m_low[i] = low
+    vt = []
+    for n in range(pieces):
+        part = slice(n * width, (n + 1) * width)
+        with region(f"wait_v{n}"):
+            v_loads[n].wait()
+        v = split(jnp.concatenate([vt_ref[level, :, part] for level in order], 0))
+        vt.append(v)
+        with region(f"wait_leaf{n}"):
+            leaf_loads[n].wait()
+        with region(f"m{n}"):
+            high, low = split(leaf[part])
+            a_high[part, :lf] = high
+            a_low[part, :lf] = low
+            for i in range(n * blocks // pieces, (n + 1) * blocks // pieces):
+                rows = slice(i * lf, (i + 1) * lf)
+                cols = slice(i * lf - n * width, (i + 1) * lf - n * width)
+                high, low = split(dot3([x[:, cols] for x in v], (a_high[rows, :lf], a_low[rows, :lf])))
+                m_high[i] = high
+                m_low[i] = low
+    vt = [jnp.concatenate(x, 1) for x in zip(*vt)]
     with region("wait_u"):
         u_load.wait()
         for copy in core_loads:
@@ -259,7 +268,7 @@
         high, low = split(rbuf[c])
         r_high[c] = high
         r_low[c] = low
-        parts, later = [], []
+        parts = []
         for i in range(blocks):
             rows = slice(i * lf, (i + 1) * lf)
             parts.append(dot3((m_high[i], m_low[i]), (r_high[c, rows, :], r_low[c, rows, :])))
@@ -272,7 +281,8 @@
                 both = split(jnp.concatenate([b[top:], a[top:]], 0))
                 change = dotk([ref[k, 2 * rank :] for ref in ch_refs[n]], both)
                 start = local_offset(level, bits, rank) + 2 * rank * k
-                later.append((start, n, k, both))
+                for ref, value in zip(both_refs, both):
+                    ref[c, start : start + 2 * rank] = value
                 merged.append(a[:top] + b[:top] - change)
             parts = merged
         p = parts[0]
@@ -280,10 +290,6 @@
         first_out[c] = jnp.where(upper, low, high)
         first_copy[c] = send(first_out.at[c], first_in.at[c], first_sem.at[c], partner(0))
         keep[c] = jnp.where(upper, high, low)
-        for start, n, k, both in later:
-            ql_ref[c, start : start + 2 * rank] = dotk(
-                [ref[k, : 2 * rank] for ref in ch_refs[n]], both
-            )
 
     def bases():
         def turned(rows, width):
@@ -301,6 +307,12 @@
         u_low[...] = low
 
     def leaves(c):
+        images = []
+        for n, level in enumerate(local_levels):
+            for k in range(2 ** (level - bits)):
+                start = local_offset(level, bits, rank) + 2 * rank * k
+                both = [ref[c, start : start + 2 * rank] for ref in both_refs]
+                images.append(split(dotk([ref[k, : 2 * rank] for ref in ch_refs[n]], both)))
         for i in range(blocks):
             rows = slice(i * lf, (i + 1) * lf)
             highs, lows = [r_high[c, rows, :]], [r_low[c, rows, :]]
@@ -308,9 +320,10 @@
             for level in local_levels:
                 place = rank * (i * 2 ** (level - bits + 1) // blocks)
                 start = local_offset(level, bits, rank) + place
-                high, low = split(ql_ref[c, start : start + rank])
-                highs.append(high)
-                lows.append(low)
+                high, low = images[start // (2 * rank)]
+                part = slice(start % (2 * rank), start % (2 * rank) + rank)
+                highs.append(high[part])
+                lows.append(low[part])
                 width += rank
             if a_high.shape[1] > width:
                 zero = jnp.zeros((a_high.shape[1] - width, CHUNK), BF16)
@@ -418,12 +431,14 @@
         x_ref[c] = x_ref[c] + dot3((u_high[...], u_low[...]), split(q))
 
     parts = {f.__name__: f for f in (forward, operator, bases, step, give, leaves, apply)}
+    early = (child(bits - 1) == 0) & (child(0) == 0)
+    groups = {True: second, False: ~second, "late": ~early, "early": early}
     for where, name, *args in schedule(bits, chunks):
         with region(name + "_".join(str(a) for a in args)):
             if where is None:
                 parts[name](*args)
             else:
-                pl.when(second == where)(functools.partial(parts[name], *args))
+                pl.when(groups[where])(functools.partial(parts[name], *args))
     with region("qwait"):
         for c in range(chunks - LATE, chunks):
             q_late[c - chunks + LATE] = gathered(c)
@@ -461,14 +476,15 @@
         pltpu.VMEM((levels, rank, rows_dev), F32),
         pltpu.VMEM((levels, rank, rows_dev), F32),
         pltpu.VMEM((bits, 2 * rank, 2 * rank), F32),
-        pltpu.SemaphoreType.DMA((4 + len(local_levels) + chunks,)),
+        pltpu.SemaphoreType.DMA((6 + len(local_levels) + chunks,)),
         pltpu.VMEM((chunks, rows_dev, CHUNK), BF16),
         pltpu.VMEM((chunks, rows_dev, CHUNK), BF16),
         pltpu.VMEM((rows_dev, depth), BF16),
         pltpu.VMEM((rows_dev, depth), BF16),
         pltpu.VMEM((blocks, levels * rank, lf), BF16),
         pltpu.VMEM((blocks, levels * rank, lf), BF16),
-        pltpu.VMEM((chunks, max(rank * (2 * blocks - 2), rank), CHUNK), F32),
+        pltpu.VMEM((chunks, max(rank * (2 * blocks - 2), rank), CHUNK), BF16),
+        pltpu.VMEM((chunks, max(rank * (2 * blocks - 2), rank), CHUNK), BF16),
         pltpu.VMEM((bits, rank * (bits + 1), 2 * rank), BF16),
         pltpu.VMEM((bits, rank * (bits + 1), 2 * rank), BF16),
         pltpu.VMEM((bits - 1, rest, gram_cols), F32),

time: 31 us -> 30 us (0.968)
  Pallas kernels: 30.8 us -> 29.6 us
    pallas_call x1, Pallas kernels: 28.7 us -> 27.5 us  [tree(): pl.pallas_call(functools.partial(tree_kernel, bits, levels, blocks), out_...]
where the time goes in v4:
time: 30 us; the launch traced here: 29.8 us
  Pallas kernels  29.6 us (99%)
    pallas_call x1, Pallas kernels, tree(): pl.pallas_call(functools.partial(tree_kernel, bits, levels, blocks), out_...  27.5 us
    pallas_call x1, Pallas kernels, finish(): pl.pallas_call(finish_kernel, out_shape=jax.ShapeDtypeStruct((rows_dev, c...  2.09 us

profile of v4, /device:TPU:0, one launch (start us, length us, event | category | flops | bytes accessed | tf_op | source)
XLA Modules:
  0.0 29.8 jit_solution(16378338515319830795)
XLA Ops:
  0.0 27.5 %tree.1 = (f32[4,1024,256]{2,1,0:T(8,128)S(1)}, f32[2,192,256]{2,1,0:T(8,128)S(1)}, bf16[1024,256]{1,0:T(8,128)(2,1)S(1)}, bf16[1024,256]{1,0:T(8,128)(2,1)S(1)}) custom-call(f32[1024,1024]{1,0:T(8,128)} %right_hbm.1, f32[1024,256]{1,0:T(8,128)} %leaf_hbm.1, f32[5,64,1024]{2,1,0:T(8,128)} %bitcast.2, f32[5,64,1024]{2,1,0:T(8,128)} %bitcast.3, ...), custom_call_target="tpu_custom_call" | custom-call | tf_op jit(solution)/shard_map/tree/pallas_call | solution.py:513
  27.6 2.1 %finish.1 = f32[1024,1024]{1,0:T(8,128)} custom-call(f32[4,1024,256]{2,1,0:T(8,128)S(1)} %get-tuple-element.9.x_ref, f32[2,192,256]{2,1,0:T(8,128)S(1)} %get-tuple-element.10.q_ref, bf16[1024,256]{1,0:T(8,128)(2,1)S(1)} %get-tuple-element.11.uh_ref, bf16[1024,256]{1,0:T(8,128)(2,1)S(1)} %get-tuple-element.12.ul_ref), custom_call_target="tpu_custom_call" | custom-call | tf_op jit(solution)/shard_map/finish/pallas_call | solution.py:558

commit v5 on v4

--- a/solution.py
+++ b/solution.py
@@ -65,18 +65,19 @@
 def schedule(bits, chunks):
     if bits == 3 and chunks == 4:
         return [
-            (None, "forward", 0), (True, "bases"), (None, "forward", 1), (None, "operator", 0),
-            (True, "leaves", 0), (None, "forward", 2), (None, "step", 0, 0), (None, "forward", 3),
-            (None, "step", 0, 1), (None, "operator", 1), (False, "bases"), (None, "step", 1, 0),
-            (None, "step", 0, 2), (False, "leaves", 3), (None, "step", 0, 3),
-            (None, "give", 0, 0), (None, "give", 1, 0), (None, "give", 0, 1),
-            (None, "step", 1, 1), (True, "leaves", 3), (False, "leaves", 2), (None, "give", 0, 2),
-            (None, "give", 0, 3), (None, "give", 1, 1), (None, "operator", 2),
-            (None, "step", 1, 2), (None, "give", 1, 2), (None, "step", 2, 0),
+            (None, "forward", 0), (True, "bases"), (None, "forward", 1), (None, "forward", 2),
+            (None, "operator", 0), (True, "leaves", 0), (None, "step", 0, 0),
+            (None, "forward", 3), (None, "step", 0, 1), (None, "operator", 1), (False, "bases"),
+            (None, "step", 1, 0), (None, "step", 0, 2), (False, "leaves", 3),
+            (None, "step", 0, 3), (None, "give", 0, 0), (None, "give", 1, 0),
+            (None, "give", 0, 1), (None, "step", 1, 1), (True, "leaves", 3), (False, "leaves", 2),
+            (None, "give", 0, 2), (None, "give", 0, 3), (None, "give", 1, 1),
+            (None, "operator", 2), (None, "step", 1, 2), (None, "step", 2, 0),
             (None, "give", 2, 0), (True, "leaves", 2), (False, "leaves", 1), (None, "step", 1, 3),
-            (True, "leaves", 1), (False, "leaves", 0), (None, "step", 2, 1), (None, "give", 1, 3),
-            (None, "give", 2, 1), ("early", "apply", 0), (None, "step", 2, 2),
-            (None, "give", 2, 2), ("late", "apply", 0), (None, "apply", 1), (None, "step", 2, 3),
+            (None, "give", 1, 2), (True, "leaves", 1), (False, "leaves", 0), (None, "step", 2, 1),
+            (None, "give", 2, 1), (None, "give", 1, 3), ("early", "apply", 0),
+            (None, "step", 2, 2), (None, "give", 2, 2), ("late", "apply", 0), (None, "apply", 1),
+            (None, "step", 2, 3),
         ]
     order = [("forward", c) for c in range(chunks)]
     order += [("operator", s) for s in range(bits)] + [("bases",)]
@@ -148,9 +149,13 @@
         count = 2 ** (level - bits)
         src = cores_hbm.at[pl.ds(2**level - 1 + me * count, count)]
         core_loads.append(load(src, core_l[n]))
-    right_loads = [
-        load(right_hbm.at[:, pl.ds(c * CHUNK, CHUNK)], rbuf.at[c]) for c in range(chunks)
-    ]
+    right_loads = {0: load(right_hbm.at[:, pl.ds(0, CHUNK)], rbuf.at[0])}
+    for c in range(1, chunks):
+        src = right_hbm.at[:, pl.ds(c * CHUNK, CHUNK)]
+        pltpu.make_async_copy(src, rbuf.at[c], sem_in.at[slots[0]]).start()
+    others = rbuf.at[pl.ds(1, chunks - 1)]
+    right_loads[1] = pltpu.make_async_copy(others, others, sem_in.at[slots[0]])
+    slots[0] += 1
     for s in range(bits):
         src = cores_hbm.at[2 ** (bits - 1 - s) - 1 + me // 2 ** (s + 1)]
         pltpu.make_async_copy(src, core_g.at[s], sem_in.at[slots[0]]).start()
@@ -264,7 +269,8 @@
     first_copy, later_copy, last_copy = {}, {}, []
 
     def forward(c):
-        right_loads[c].wait()
+        if c in right_loads:
+            right_loads[c].wait()
         high, low = split(rbuf[c])
         r_high[c] = high
         r_low[c] = low
@@ -476,7 +482,7 @@
         pltpu.VMEM((levels, rank, rows_dev), F32),
         pltpu.VMEM((levels, rank, rows_dev), F32),
         pltpu.VMEM((bits, 2 * rank, 2 * rank), F32),
-        pltpu.SemaphoreType.DMA((6 + len(local_levels) + chunks,)),
+        pltpu.SemaphoreType.DMA((8 + len(local_levels),)),
         pltpu.VMEM((chunks, rows_dev, CHUNK), BF16),
         pltpu.VMEM((chunks, rows_dev, CHUNK), BF16),
         pltpu.VMEM((rows_dev, depth), BF16),
@@ -523,15 +529,12 @@
     )(right_side, leaf_inverse, vt, ut, cores)
 
 
-def finish_kernel(x_ref, q_ref, uh_ref, ul_ref, out_hbm, last, sems):
+def finish_kernel(x_ref, q_ref, uh_ref, ul_ref, out_hbm, last, sem):
     chunks, rows_dev, width = x_ref.shape
-    copies = []
 
     def write(src, rows, c):
         dst = out_hbm.at[pl.ds(rows, src.shape[0]), pl.ds(c * width, width)]
-        copy = pltpu.make_async_copy(src, dst, sems.at[len(copies)])
-        copy.start()
-        copies.append(copy)
+        pltpu.make_async_copy(src, dst, sem.at[0]).start()
 
     late = q_ref.shape[0]
     for c in range(chunks - late):
@@ -548,8 +551,7 @@
             rows = slice(start, start + piece)
             last[n, rows] = x_ref[c, rows] + dot3((uh_ref[rows], ul_ref[rows]), q)
             write(last.at[n, pl.ds(start, piece)], start, c)
-    for copy in copies:
-        copy.wait()
+    pltpu.make_async_copy(x_ref, x_ref, sem.at[0]).wait()
 
 
 def finish(x, q, u_high, u_low):
@@ -562,7 +564,7 @@
         out_specs=pl.BlockSpec(memory_space=pltpu.HBM),
         scratch_shapes=[
             pltpu.VMEM((q.shape[0], rows_dev, width), F32),
-            pltpu.SemaphoreType.DMA((chunks + q.shape[0] * (PIECES - 1),)),
+            pltpu.SemaphoreType.DMA((1,)),
         ],
         compiler_params=pltpu.CompilerParams(vmem_limit_bytes=FINISH_VMEM),
         name="finish",

time: 30 us -> 29.9 us (level)
  no operation moved by 1% of the time
where the time goes in v5:
time: 29.9 us; the launch traced here: 29.7 us
  Pallas kernels  29.5 us (99%)
    pallas_call x1, Pallas kernels, tree(): pl.pallas_call(functools.partial(tree_kernel, bits, levels, blocks), out_...  27.5 us
    pallas_call x1, Pallas kernels, finish(): pl.pallas_call(finish_kernel, out_shape=jax.ShapeDtypeStruct((rows_dev, c...  2.05 us

profile of v5, /device:TPU:0, one launch (start us, length us, event | category | flops | bytes accessed | tf_op | source)
XLA Modules:
  0.0 29.7 jit_solution(10602439468737754554)
XLA Ops:
  0.0 27.5 %tree.1 = (f32[4,1024,256]{2,1,0:T(8,128)S(1)}, f32[2,192,256]{2,1,0:T(8,128)S(1)}, bf16[1024,256]{1,0:T(8,128)(2,1)S(1)}, bf16[1024,256]{1,0:T(8,128)(2,1)S(1)}) custom-call(f32[1024,1024]{1,0:T(8,128)} %right_hbm.1, f32[1024,256]{1,0:T(8,128)} %leaf_hbm.1, f32[5,64,1024]{2,1,0:T(8,128)} %bitcast.2, f32[5,64,1024]{2,1,0:T(8,128)} %bitcast.3, ...), custom_call_target="tpu_custom_call" | custom-call | tf_op jit(solution)/shard_map/tree/pallas_call | solution.py:519
  27.5 2.0 %finish.1 = f32[1024,1024]{1,0:T(8,128)} custom-call(f32[4,1024,256]{2,1,0:T(8,128)S(1)} %get-tuple-element.9.x_ref, f32[2,192,256]{2,1,0:T(8,128)S(1)} %get-tuple-element.10.q_ref, bf16[1024,256]{1,0:T(8,128)(2,1)S(1)} %get-tuple-element.11.uh_ref, bf16[1024,256]{1,0:T(8,128)(2,1)S(1)} %get-tuple-element.12.ul_ref), custom_call_target="tpu_custom_call" | custom-call | tf_op jit(solution)/shard_map/finish/pallas_call | solution.py:560

commit v6 on v4

--- a/solution.py
+++ b/solution.py
@@ -67,15 +67,15 @@
         return [
             (None, "forward", 0), (True, "bases"), (None, "forward", 1), (None, "operator", 0),
             (True, "leaves", 0), (None, "forward", 2), (None, "step", 0, 0), (None, "forward", 3),
-            (None, "step", 0, 1), (None, "operator", 1), (False, "bases"), (None, "step", 1, 0),
-            (None, "step", 0, 2), (False, "leaves", 3), (None, "step", 0, 3),
-            (None, "give", 0, 0), (None, "give", 1, 0), (None, "give", 0, 1),
+            (None, "give", 0, 0), (None, "step", 0, 1), (None, "operator", 1), (False, "bases"),
+            (None, "step", 1, 0), (None, "step", 0, 2), (False, "leaves", 3),
+            (None, "step", 0, 3), (None, "give", 1, 0), (None, "give", 0, 1),
             (None, "step", 1, 1), (True, "leaves", 3), (False, "leaves", 2), (None, "give", 0, 2),
-            (None, "give", 0, 3), (None, "give", 1, 1), (None, "operator", 2),
+            (None, "give", 1, 1), (None, "give", 0, 3), (None, "operator", 2),
             (None, "step", 1, 2), (None, "give", 1, 2), (None, "step", 2, 0),
             (None, "give", 2, 0), (True, "leaves", 2), (False, "leaves", 1), (None, "step", 1, 3),
-            (True, "leaves", 1), (False, "leaves", 0), (None, "step", 2, 1), (None, "give", 1, 3),
-            (None, "give", 2, 1), ("early", "apply", 0), (None, "step", 2, 2),
+            (True, "leaves", 1), (False, "leaves", 0), (None, "step", 2, 1), (None, "give", 2, 1),
+            (None, "give", 1, 3), ("early", "apply", 0), (None, "step", 2, 2),
             (None, "give", 2, 2), ("late", "apply", 0), (None, "apply", 1), (None, "step", 2, 3),
         ]
     order = [("forward", c) for c in range(chunks)]

time: 30 us -> 30 us (level)
  no operation moved by 1% of the time
where the time goes in v6:
time: 30 us; the launch traced here: 29.9 us
  Pallas kernels  29.7 us (99%)
    pallas_call x1, Pallas kernels, tree(): pl.pallas_call(functools.partial(tree_kernel, bits, levels, blocks), out_...  27.6 us
    pallas_call x1, Pallas kernels, finish(): pl.pallas_call(finish_kernel, out_shape=jax.ShapeDtypeStruct((rows_dev, c...  2.09 us

profile of v6, /device:TPU:0, one launch (start us, length us, event | category | flops | bytes accessed | tf_op | source)
XLA Modules:
  0.0 29.9 jit_solution(11812405921971717230)
XLA Ops:
  0.0 27.6 %tree.1 = (f32[4,1024,256]{2,1,0:T(8,128)S(1)}, f32[2,192,256]{2,1,0:T(8,128)S(1)}, bf16[1024,256]{1,0:T(8,128)(2,1)S(1)}, bf16[1024,256]{1,0:T(8,128)(2,1)S(1)}) custom-call(f32[1024,1024]{1,0:T(8,128)} %right_hbm.1, f32[1024,256]{1,0:T(8,128)} %leaf_hbm.1, f32[5,64,1024]{2,1,0:T(8,128)} %bitcast.2, f32[5,64,1024]{2,1,0:T(8,128)} %bitcast.3, ...), custom_call_target="tpu_custom_call" | custom-call | tf_op jit(solution)/shard_map/tree/pallas_call | solution.py:513
  27.6 2.1 %finish.1 = f32[1024,1024]{1,0:T(8,128)} custom-call(f32[4,1024,256]{2,1,0:T(8,128)S(1)} %get-tuple-element.9.x_ref, f32[2,192,256]{2,1,0:T(8,128)S(1)} %get-tuple-element.10.q_ref, bf16[1024,256]{1,0:T(8,128)(2,1)S(1)} %get-tuple-element.11.uh_ref, bf16[1024,256]{1,0:T(8,128)(2,1)S(1)} %get-tuple-element.12.ul_ref), custom_call_target="tpu_custom_call" | custom-call | tf_op jit(solution)/shard_map/finish/pallas_call | solution.py:558
